TPU v7x, 512 devices: a whole 4x4x16 slice. The times are simulated.
512 devices in a mesh: tm: 32 (over z, core), row: 16 (over x, y).
Axes of the slice: x: 4, y: 4, z: 16, core: 2. Of those that a mesh axis runs over, the one named last changes fastest.
Arguments:
- video: bfloat16 [32, 4, 384, 1024], P('tm', None, 'row'), may hold values from -6 to 6
- stem_weight: bfloat16 [64, 4, 3, 3], replicated, may hold values from -1 to 1
- w_qkv: bfloat16 [1536, 2304], P('tm'), may hold values from -0.15625 to 0.15625
- decay: float32 [32, 6], P('tm'), may hold values from 0.04 to 1, as said below
Outputs:
- mixed: bfloat16 [32, 32, 128, 768], P('tm', 'row')
Inputs may be any that keep to these rules, and one draw needn't show every extreme that they name: decay lies in (0, 1].
All inputs are finite; a program needn't handle non-finite values.
Results may differ from a plain program's by a relative error of at most 0.012.
Values may be sent and summed in bfloat16 or wider, within the bound.
A program may use at most 128 MiB of HBM per device.

v0:
```python
import jax
import jax.numpy as jnp
from jax import lax
from jax.sharding import PartitionSpec as P

HEADS = 6


def shifted(block, axis, distance):
    devices = range(lax.axis_size(axis))
    route = [(i - distance, i) for i in devices if i - distance in devices]
    return lax.ppermute(block, axis, route)


def prefix_2(x, axis, join, neutral):
    place = lax.axis_index(axis)
    gathered = jax.tree.map(
        lambda a, kind: lax.all_gather(a.astype(kind), axis), x, (jnp.bfloat16, jnp.bfloat16)
    )
    state = jax.tree.map(lambda a, e: jnp.zeros_like(a) + jnp.asarray(e, a.dtype), x, neutral)

    def one(step, state):
        return join(
            state,
            jax.tree.map(
                lambda a, own: lax.dynamic_index_in_dim(a, step, 0, False).astype(own.dtype),
                gathered,
                x,
            ),
        )

    return lax.fori_loop(0, place, one, state)


def combine(first_pair, later_pair):
    return (first_pair[0] * later_pair[0], later_pair[0] * first_pair[1] + later_pair[1])


def summarize(frame_rates, outer_sums):
    factor = jnp.ones_like(frame_rates[0])
    summed = jnp.zeros_like(outer_sums[0])
    factor = factor * frame_rates[0]
    summed = frame_rates[0] * summed + outer_sums[0]
    return (factor, summed)


def unroll(prefix, frame_rates, outer_sums):
    running = prefix
    running = frame_rates[0] * running + outer_sums[0]
    collected = [running]
    return jnp.stack(collected, axis=0)


def local(video, stem_weight, w_qkv, decay):
    frames_dev = video.shape[0]
    upper_row = shifted(video[:, :, -1:, :], "row", 1)
    padded = jnp.concatenate([upper_row, video], axis=2)
    padded = jnp.pad(padded, ((0, 0), (0, 0), (0, 0), (1, 0)))
    stem_out = lax.conv_general_dilated(
        padded,
        stem_weight,
        (2, 2),
        "VALID",
        dimension_numbers=("NCHW", "OIHW", "NCHW"),
        preferred_element_type=jnp.float32,
    )
    features = jnp.tanh(stem_out).astype(jnp.bfloat16)
    channels = features.shape[1]
    patch_rows = features.shape[2] // 6
    patch_cols = features.shape[3] // 4
    frame_tokens = patch_rows * patch_cols
    shaped = features.reshape(frames_dev, channels, patch_rows, 6, patch_cols, 4).transpose(
        0, 2, 4, 1, 3, 5
    )
    tokens = shaped.reshape(frames_dev * frame_tokens, channels * 24)
    qkv_width = w_qkv.shape[1]
    empty = jnp.zeros((tokens.shape[0], qkv_width), jnp.float32)
    block_rows = lax.all_gather(w_qkv, "tm", axis=0, tiled=True)
    columns = lax.slice_in_dim(tokens, 0, block_rows.shape[0], axis=1)
    projected = (empty + jnp.dot(columns, block_rows, preferred_element_type=jnp.float32)).astype(
        jnp.bfloat16
    )
    inner_width = qkv_width // 3
    head_size = inner_width // HEADS
    queries = projected[:, :inner_width].reshape(frames_dev, frame_tokens, HEADS, head_size)
    keys = projected[:, inner_width : 2 * inner_width].reshape(
        frames_dev, frame_tokens, HEADS, head_size
    )
    values = projected[:, 2 * inner_width :].reshape(frames_dev, frame_tokens, HEADS, head_size)
    kv_local = jnp.einsum("fnhd,fnhe->fhde", keys, values, preferred_element_type=jnp.float32)
    head_rates = decay[:, :, None, None]
    kv_total = lax.psum(kv_local.astype(jnp.bfloat16), "row").astype(jnp.float32)
    factor, summed = summarize(head_rates, kv_total)
    prefix = prefix_2(
        (factor, summed), "tm", combine, (jnp.ones_like(factor), jnp.zeros_like(summed))
    )[1]
    states = unroll(prefix, head_rates, kv_total).astype(jnp.bfloat16)
    attended = jnp.einsum("fnhd,fhde->fnhe", queries, states, preferred_element_type=jnp.float32)
    attended = attended * lax.rsqrt(jnp.mean(attended * attended, axis=-1, keepdims=True) + 1e-06)
    return attended.reshape(frames_dev, patch_rows, patch_cols, inner_width).astype(jnp.bfloat16)


def solution(mesh):
    return jax.shard_map(
        local,
        mesh=mesh,
        in_specs=(P("tm", None, "row", None), P(), P("tm", None), P("tm", None)),
        out_specs=P("tm", "row", None, None),
        check_vma=False,
    )
```

profile of v0, /device:TPU:481, one launch (start us, length us, event | category | flops | bytes accessed | tf_op | source)
XLA Modules:
  0.0 324.3 jit_solution(5156422705934072437)
XLA Ops:
  6.5 0.7 all-gather.5.cloned.1.call-update
  7.3 0.9 slice.12
  8.2 3.2 collective-permute-start
  11.4 0.9 collective-permute-done
  12.2 1.0 maximum_bitcast_fusion
  13.2 0.1 pad.2
  13.4 1.3 reshape.102
  14.7 4.3 %copy.74 = bf16[4,25,1,8,130]{3,0,4,1,2:T(4,128)(2,1)S(1)} copy(bf16[4,25,1,8,130]{4,3,1,0,2:T(8,128)(2,1)} %reshape.102) | data formatting | bytes 416000 | tf_op jit(solution)/shard_map/conv_general_dilated | solution.py:59
  19.0 0.1 slice.18
  19.1 5.0 %fusion.3 = f32[12,8,65,64]{3,1,2,0:T(8,128)} fusion(bf16[64,4,3,3]{0,1,3,2:T(4,128)(2,1)S(1)} %copy-done, bf16[4,25,1,7,2]{3,0,4,1,2:T(4,128)(2,1)S(1)} %slice.18, bf16[4,25,1,8,130]{3,0,4,1,2:T(4,128)(2,1)S(1)} %copy.74), kind=kOutput, calls=%fused_computation.7 | convolution fusion | flops 29387520 | bytes 1812848 | tf_op jit(solution)/shard_map/conv_general_dilated | solution.py:59
  24.1 3.3 %copy.75 = f32[12,8,65,64]{2,3,1,0:T(8,128)S(1)} copy(f32[12,8,65,64]{3,1,2,0:T(8,128)} %fusion.3) | data formatting | bytes 3194880 | tf_op jit(solution)/shard_map/conv_general_dilated | solution.py:59
  27.4 0.5 tanh_convert_fusion
  27.9 1.2 copy.76
  29.2 1.2 reshape.91
  30.4 0.9 copy.77
  31.3 1.3 copy.78
  32.6 52.8 %all-gather.5.cloned.1.call-done = bf16[1536,2304]{1,0:T(8,128)(2,1)} async-done(((bf16[48,2304]{1,0:T(8,128)(2,1)}), bf16[1536,2304]{1,0:T(8,128)(2,1)}) %all-gather.5.cloned.1.call-update) | async-done | bytes 7077904 | tf_op jit(solution)/shard_map/all_gather | solution.py:78
  85.3 5.0 %convolution_convert_fusion = bf16[256,2304]{1,0:T(8,128)(2,1)S(1)} fusion(bf16[1536,2304]{1,0:T(8,128)(2,1)} %all-gather.5.cloned.1.call-done, bf16[192,8,2,128]{3,2,1,0:T(2,128)(2,1)S(1)} %bitcast.66), kind=kOutput, calls=%fused_computation.4 | convolution fusion | flops 1812529152 | bytes 9043968 | tf_op jit(solution)/shard_map/dot_general | solution.py:80
  90.5 0.2 copy.79
  90.6 0.2 copy.80
  90.8 0.9 fusion.6
  91.9 110.7 %all-reduce.2.cloned.1.call-done = bf16[1,6,128,128]{3,2,1,0:T(8,128)(2,1)} async-done(((bf16[1,6,128,128]{3,2,1,0:T(8,128)(2,1)}), bf16[1,6,128,128]{3,2,1,0:T(8,128)(2,1)}) %all-reduce.2.cloned.1.call-update) | async-done | bytes 196624 | tf_op jit(solution)/shard_map/psum | solution.py:92
  202.5 1.7 fusion.9
  204.3 30.0 %all-gather.1 = bf16[32,1,6]{2,1,0:T(2,128)(2,1)S(1)} all-gather(bf16[1,1,6]{2,1,0:T(2,128)(2,1)S(1)} %convert_bitcast_fusion.1), channel_id=2, replica_groups=mesh['tm'=32,'row'=16] {'tm'}, dimensions={0}, use_global_device_ids=true | all-gather | bytes 396 | tf_op jit(solution)/shard_map/all_gather | solution.py:18
  234.3 0.1 copy.71
  234.4 0.1 copy.82
  234.5 0.2 copy.83
  234.7 47.0 %all-gather.7.cloned.1.call-done = bf16[32,6,128,128]{3,2,1,0:T(8,128)(2,1)} async-done(((bf16[1,6,128,128]{3,2,1,0:T(8,128)(2,1)}), bf16[32,6,128,128]{3,2,1,0:T(8,128)(2,1)}) %all-gather.7.cloned.1.call-update) | async-done | bytes 6291472 | tf_op jit(solution)/shard_map/all_gather | solution.py:18
  281.7 34.4 %while.12 = (s32[]{:T(128)}, f32[6,128,128]{2,1,0:T(8,128)S(1)}, s32[]{:T(128)}, bf16[32,6,1,1]{1,3,2,0:T(2,128)(2,1)S(1)}, bf16[32,6,128,128]{3,2,1,0:T(8,128)(2,1)}, /*index=5*/s32[]{:T(128)}, s32[]{:T(128)}, s32[]{:T(128)}) while((s32[]{:T(128)}, f32[6,128,128]{2,1,0:T(8,128)S(1)}, s32[]{:T(128)}, bf16[32,6,1,1]{1,3,2,0:T(2,128)(2,1)S(1)}, ...), condition=%wide.region_2.3_spmd, body=%wide.region_1.2_spmd.sunk | while | flops 294923 | bytes 983227 | solution.py:32
  281.7 1.1 convert_add_fusion.3
  282.8 1.1 convert_add_fusion.3
  283.9 1.1 convert_add_fusion.3
  285.0 1.1 convert_add_fusion.3
  286.2 1.1 convert_add_fusion.3
  287.3 1.1 convert_add_fusion.3
  288.4 1.1 convert_add_fusion.3
  289.5 1.1 convert_add_fusion.3
  290.6 1.1 convert_add_fusion.3
  291.7 1.1 convert_add_fusion.3
  292.8 1.1 convert_add_fusion.3
  293.9 1.1 convert_add_fusion.3
  295.0 1.1 convert_add_fusion.3
  296.1 1.1 convert_add_fusion.3
  297.3 1.1 convert_add_fusion.3
  298.4 1.1 convert_add_fusion.3
  299.5 1.1 convert_add_fusion.3
  300.6 1.1 convert_add_fusion.3
  301.7 1.1 convert_add_fusion.3
  302.8 1.1 convert_add_fusion.3
  303.9 1.1 convert_add_fusion.3
  305.0 1.1 convert_add_fusion.3
  306.1 1.1 convert_add_fusion.3
  307.3 1.1 convert_add_fusion.3
  308.4 1.1 convert_add_fusion.3
  309.5 1.1 convert_add_fusion.3
  310.6 1.1 convert_add_fusion.3
  311.7 1.1 convert_add_fusion.3
  312.8 1.1 convert_add_fusion.3
  313.9 1.1 convert_add_fusion.3
  315.0 1.1 convert_add_fusion.3
  316.1 0.4 multiply_reduce_fusion
  316.5 0.1 multiply_convert_fusion
  316.6 0.1 convert_element_type.83
  316.7 1.0 copy.86
  (50 shorter events, 0.6 us)
Async XLA Ops:
  6.5 12.6 %copy-start = (bf16[64,4,3,3]{0,1,3,2:T(4,128)(2,1)S(1)}, bf16[64,4,3,3]{0,1,3,2:T(4,128)(2,1)}, u32[]{:S(2)}) copy-start(bf16[64,4,3,3]{0,1,3,2:T(4,128)(2,1)} %param.7) | copy-start | bytes 13828
  6.5 78.8 %all-gather.5.cloned.1.call-start = ((), (), s32[]{:S(2)}) async-start(), calls=%async_computation | async-start | bytes 7299072 | tf_op jit(solution)/shard_map/all_gather | solution.py:78
  7.3 195.3 %all-reduce.2.cloned.1.call-start = ((), (), s32[]{:S(2)}) async-start(), calls=%async_computation.1 | async-start | bytes 393216 | tf_op jit(solution)/shard_map/psum | solution.py:92
  8.2 4.1 %collective-permute-start = (bf16[1,4,1,1024]{3,2,1,0:T(2,128)(2,1)S(1)}, bf16[1,4,1,1024]{3,2,1,0:T(2,128)(2,1)S(1)}, u32[]{:S(2)}, u32[]{:S(2)}) collective-permute-start(bf16[1,4,1,1024]{3,2,1,0:T(2,128)(2,1)S(1)} %slice.12), channel_id=1, source_target_pairs={{0,1},{1,2},{2,3},{3,4},{4,5},{5,6},{6,7},{7,8},{8,9},{9,10},{10,1... | collective-permute-start | bytes 24584 | tf_op jit(solution)/shard_map/ppermute | solution.py:12
  24.1 3.3 %copy-start.2 = (pred[8,65]{1,0:T(8,128)(4,1)S(1)}, pred[8,65]{1,0:T(8,128)(4,1)}, u32[]{:S(2)}) copy-start(pred[8,65]{1,0:T(8,128)(4,1)} %constant.40) | copy-start | bytes 1564
  90.4 1.5 copy-start.3
  91.8 189.9 %all-gather.7.cloned.1.call-start = ((), (), s32[]{:S(2)}) async-start(), calls=%async_computation.2 | async-start | bytes 6488064 | tf_op jit(solution)/shard_map/all_gather | solution.py:18
  204.2 111.9 %copy-start.1 = (bf16[1,6,128,128]{3,2,1,0:T(8,128)(2,1)S(1)}, bf16[1,6,128,128]{3,2,1,0:T(8,128)(2,1)}, u32[]{:S(2)}) copy-start(bf16[1,6,128,128]{3,2,1,0:T(8,128)(2,1)} %all-reduce.2.cloned.1.call-done) | copy-start | bytes 589828
Sparse Core Ops, SparseCore 0:
  9.5 75.7 all-gather.4
  91.9 110.5 all-reduce.1
  204.6 76.9 all-gather.6
where the time goes:
time: 326 us; the launch traced here: 324 us
  waiting for transfers between devices  212 us (65%)
  other arithmetic  36.6 us (11%)
  blocking collectives  30 us (9%)
  local copies, waits for them, and re-layouts  16.6 us (5%)
  between operations  13.3 us (4%)
  matrix products  11.4 us (3%)
  starting transfers between devices  3.28 us (1%)
    psum x1, waiting for transfers between devices, local(): lax.psum(kv_local.astype(jnp.bfloat16), 'row').astype(jnp.float32)  111 us
    all_gather x1, waiting for transfers between devices, local(): block_rows = lax.all_gather(w_qkv, 'tm', axis=0, tiled=True)  52.8 us
    all_gather x1, waiting for transfers between devices, prefix_2(): lax.all_gather(a.astype(kind), axis)  47 us
    add x31, other arithmetic, combine(): later_pair[0] * first_pair[1] + later_pair[1]  33.1 us
    all_gather x1, blocking collectives, prefix_2(): lax.all_gather(a.astype(kind), axis)  30 us
    conv_general_dilated x4, local copies, waits for them, and re-layouts, local(): lax.conv_general_dilated(padded, stem_weight, (2, 2), 'VALID', dimension_...  9.02 us
  transfers between devices with their start and end apart: 4, of which 4 were waited for; matrix products, arithmetic and copies ran while one was open for 7% of the time, Pallas kernels for 0%

commit v1 on v0

v1 whole, which is shorter than its diff:
```python
import jax
import jax.numpy as jnp
from jax import lax
from jax.experimental import pallas as pl
from jax.experimental.pallas import tpu as pltpu
from jax.sharding import PartitionSpec as P

HEADS = 6
DH = 128
ROW = 16
QUAD = 8
GROUPS = 4
SHARE = HEADS * DH // ROW
MESH = pl.DeviceIdType.MESH


def shifted(block, axis, distance):
    devices = range(lax.axis_size(axis))
    route = [(i - distance, i) for i in devices if i - distance in devices]
    return lax.ppermute(block, axis, route)


def copy_to(src, dst, sems, slot, axis, index):
    return pltpu.make_async_remote_copy(
        src_ref=src,
        dst_ref=dst,
        send_sem=sems.at[0, slot],
        recv_sem=sems.at[1, slot],
        device_id={axis: index},
        device_id_type=MESH,
    )


def attend_kernel(
    proj_ref,
    decay_ref,
    out_ref,
    kv_buf,
    part_buf,
    kv_share,
    quad_kv,
    quad_decay,
    total,
    total_decay,
    group_kv,
    group_decay,
    state_share,
    state_buf,
    row_sems,
    quad_sems,
    rate_sems,
    group_sems,
    product_sems,
    state_sems,
):
    tm = lax.axis_index("tm")
    row = lax.axis_index("row")
    group = tm // QUAD
    seat = lax.rem(tm, QUAD)
    first = group * QUAD

    row_peers = [lax.rem(row + d, ROW) for d in range(1, ROW)]
    quad_peers = [first + lax.rem(seat + d, QUAD) for d in range(1, QUAD)]
    group_peers = [lax.rem(tm + d * QUAD, QUAD * GROUPS) for d in range(1, GROUPS)]

    barrier = pltpu.get_barrier_semaphore()
    for peer in row_peers:
        pl.semaphore_signal(barrier, inc=1, device_id={"row": peer}, device_id_type=MESH)
    for peer in quad_peers + group_peers:
        pl.semaphore_signal(barrier, inc=1, device_id={"tm": peer}, device_id_type=MESH)

    width = HEADS * DH
    for h in range(HEADS):
        keys = proj_ref[:, width + h * DH : width + (h + 1) * DH]
        values = proj_ref[:, 2 * width + h * DH : 2 * width + (h + 1) * DH]
        outer = lax.dot_general(
            keys, values, (((0,), (0,)), ((), ())), preferred_element_type=jnp.float32
        )
        kv_buf[h * DH : (h + 1) * DH, :] = outer.astype(jnp.bfloat16)

    pl.semaphore_wait(barrier, ROW + QUAD + GROUPS - 3)

    def share_of(index):
        return kv_buf.at[pl.ds(pl.multiple_of(index * SHARE, 16), SHARE), :]

    sends = []
    for d in range(1, ROW):
        copy = copy_to(share_of(row_peers[d - 1]), part_buf.at[d], row_sems, d, "row", row_peers[d - 1])
        copy.start()
        sends.append(copy)
    rates = []
    for d in range(1, QUAD):
        copy = copy_to(decay_ref, quad_decay.at[d], rate_sems, d, "tm", quad_peers[d - 1])
        copy.start()
        rates.append(copy)
    quad_decay[0] = decay_ref[...]

    start = row * SHARE
    summed = kv_buf[pl.ds(pl.multiple_of(start, 16), SHARE), :].astype(jnp.float32)
    for copy in rates:
        copy.wait()

    def decay_of(offset):
        return quad_decay[offset]

    product = jnp.ones((8, 128), jnp.float32)
    for i in range(QUAD):
        product = product * quad_decay[i]
    total_decay[...] = product

    for d in range(1, ROW):
        sends[d - 1].wait()
        summed = summed + part_buf[d].astype(jnp.float32)
    kv_share[...] = summed.astype(jnp.bfloat16)

    quads = []
    for d in range(1, QUAD):
        copy = copy_to(kv_share, quad_kv.at[d], quad_sems, d, "tm", quad_peers[d - 1])
        copy.start()
        quads.append(copy)
    products = []
    for d in range(1, GROUPS):
        copy = copy_to(
            total_decay, group_decay.at[d], product_sems, d, "tm", group_peers[d - 1]
        )
        copy.start()
        products.append(copy)

    head = (start + lax.broadcasted_iota(jnp.int32, (SHARE, DH), 0)) // DH

    def expand(tile):
        factor = jnp.zeros((SHARE, DH), jnp.float32)
        for h in range(HEADS):
            factor = jnp.where(head == h, tile[h : h + 1, :], factor)
        return factor

    quad_kv[0] = kv_share[...]
    for copy in quads:
        copy.wait()

    def pass_one(i, running):
        slot = lax.rem(seat - i + QUAD, QUAD)
        return expand(quad_decay[slot]) * running + quad_kv[slot].astype(jnp.float32)

    whole = lax.fori_loop(0, QUAD, pass_one, jnp.zeros((SHARE, DH), jnp.float32))
    total[...] = whole.astype(jnp.bfloat16)

    groups = []
    for d in range(1, GROUPS):
        copy = copy_to(total, group_kv.at[d], group_sems, d, "tm", group_peers[d - 1])
        copy.start()
        groups.append(copy)
    for copy in products:
        copy.wait()
    for copy in groups:
        copy.wait()

    def pass_groups(g, running):
        slot = lax.rem(group - g + GROUPS, GROUPS)
        return expand(group_decay[slot]) * running + group_kv[slot].astype(jnp.float32)

    running = lax.fori_loop(0, group, pass_groups, jnp.zeros((SHARE, DH), jnp.float32))
    running = lax.fori_loop(0, seat + 1, pass_one, running)
    state_share[...] = running.astype(jnp.bfloat16)

    states = []
    for d in range(1, ROW):
        copy = copy_to(
            state_share, state_buf.at[row], state_sems, d, "row", row_peers[d - 1]
        )
        copy.start()
        states.append(copy)
    state_buf[row] = state_share[...]
    for copy in states:
        copy.wait_send()
    for d in range(1, ROW):
        sender = lax.rem(row - d + ROW, ROW)
        copy_to(state_share, state_buf.at[sender], state_sems, d, "row", sender).wait_recv()

    state = state_buf[...].reshape(HEADS * DH, DH)
    for h in range(HEADS):
        queries = proj_ref[:, h * DH : (h + 1) * DH]
        attended = jnp.dot(
            queries, state[h * DH : (h + 1) * DH, :], preferred_element_type=jnp.float32
        )
        scale = lax.rsqrt(jnp.mean(attended * attended, axis=-1, keepdims=True) + 1e-06)
        out_ref[:, h * DH : (h + 1) * DH] = (attended * scale).astype(jnp.bfloat16)


def attend(projected, decay_tile):
    tokens = projected.shape[0]
    bf, f32 = jnp.bfloat16, jnp.float32
    return pl.pallas_call(
        attend_kernel,
        out_shape=jax.ShapeDtypeStruct((tokens, HEADS * DH), bf),
        in_specs=[pl.BlockSpec(memory_space=pltpu.VMEM)] * 2,
        out_specs=pl.BlockSpec(memory_space=pltpu.VMEM),
        scratch_shapes=[
            pltpu.VMEM((HEADS * DH, DH), bf),
            pltpu.VMEM((ROW, SHARE, DH), bf),
            pltpu.VMEM((SHARE, DH), bf),
            pltpu.VMEM((QUAD, SHARE, DH), bf),
            pltpu.VMEM((QUAD, 8, 128), f32),
            pltpu.VMEM((SHARE, DH), bf),
            pltpu.VMEM((8, 128), f32),
            pltpu.VMEM((GROUPS, SHARE, DH), bf),
            pltpu.VMEM((GROUPS, 8, 128), f32),
            pltpu.VMEM((SHARE, DH), bf),
            pltpu.VMEM((ROW, SHARE, DH), bf),
            pltpu.SemaphoreType.DMA((2, ROW)),
            pltpu.SemaphoreType.DMA((2, QUAD)),
            pltpu.SemaphoreType.DMA((2, QUAD)),
            pltpu.SemaphoreType.DMA((2, GROUPS)),
            pltpu.SemaphoreType.DMA((2, GROUPS)),
            pltpu.SemaphoreType.DMA((2, ROW)),
        ],
        compiler_params=pltpu.CompilerParams(collective_id=0, has_side_effects=True),
        name="attend",
    )(projected, decay_tile)


def local(video, stem_weight, w_qkv, decay):
    frames_dev = video.shape[0]
    row = lax.axis_index("row")
    depth = w_qkv.shape[0] // ROW
    piece = lax.dynamic_slice_in_dim(w_qkv, row * depth, depth, axis=0)
    weights = lax.all_gather(piece, ("tm", "row"), axis=0, tiled=True)

    upper_row = shifted(video[:, :, -1:, :], "row", 1)
    padded = jnp.concatenate([upper_row, video], axis=2)
    padded = jnp.pad(padded, ((0, 0), (0, 0), (0, 0), (1, 0)))
    stem_out = lax.conv_general_dilated(
        padded,
        stem_weight,
        (2, 2),
        "VALID",
        dimension_numbers=("NCHW", "OIHW", "NCHW"),
        preferred_element_type=jnp.float32,
    )
    features = jnp.tanh(stem_out).astype(jnp.bfloat16)
    channels = features.shape[1]
    patch_rows = features.shape[2] // 6
    patch_cols = features.shape[3] // 4
    shaped = features.reshape(frames_dev, channels, patch_rows, 6, patch_cols, 4).transpose(
        0, 2, 4, 1, 3, 5
    )
    tokens = shaped.reshape(frames_dev * patch_rows * patch_cols, channels * 24)
    projected = jnp.dot(tokens, weights, preferred_element_type=jnp.float32).astype(jnp.bfloat16)
    decay_tile = jnp.pad(jnp.broadcast_to(decay.reshape(HEADS, 1), (HEADS, 128)), ((0, 2), (0, 0)))
    mixed = attend(projected, decay_tile)
    return mixed.reshape(frames_dev, patch_rows, patch_cols, HEADS * DH)


def solution(mesh):
    return jax.shard_map(
        local,
        mesh=mesh,
        in_specs=(P("tm", None, "row", None), P(), P("tm", None), P("tm", None)),
        out_specs=P("tm", "row", None, None),
        check_vma=False,
    )
```

time: 326 us -> 297 us (0.911)
  the two profiles are of different devices: /device:TPU:481 before, /device:TPU:1 now
where the time goes in v1:
time: 297 us; the launch traced here: 294 us
  waiting for transfers between devices  168 us (57%)
  local copies, waits for them, and re-layouts  39.5 us (13%)
  matrix products  37.1 us (12%)
  Pallas kernels  32 us (11%)
  between operations  13.5 us (5%)
  starting transfers between devices  4.06 us (1%)
    all_gather x1, waiting for transfers between devices, local(): weights = lax.all_gather(piece, ('tm', 'row'), axis=0, tiled=True)  168 us
    unnamed x11, local copies, waits for them, and re-layouts  36.2 us
    pallas_call x1, Pallas kernels, attend(): pl.pallas_call(attend_kernel, out_shape=jax.ShapeDtypeStruct((tokens, HEA...  32 us
    conv_general_dilated x1, matrix products, local(): lax.conv_general_dilated(padded, stem_weight, (2, 2), 'VALID', dimension_...  31 us
    dot_general x1, matrix products, local(): jnp.dot(tokens, weights, preferred_element_type=jnp.float32)  6.08 us
  transfers between devices with their start and end apart: 2, of which 1 were waited for; matrix products, arithmetic and copies ran while one was open for 17% of the time, Pallas kernels for 0%

profile of v1, /device:TPU:1, one launch (start us, length us, event | category | flops | bytes accessed | tf_op | source)
XLA Modules:
  0.0 294.2 jit_solution(1240629253817416446)
XLA Ops:
  6.5 0.0 copy-start
  6.5 0.0 copy-start.2
  6.5 0.0 copy-start.1
  6.5 0.0 all-gather.3.cloned.1.call-start
  6.6 0.9 copy-done
  7.5 0.6 dynamic-slice_bitcast_fusion
  8.1 0.0 all-gather.3.cloned.1.call-update
  8.1 0.9 slice.3
  9.0 0.5 copy.14
  9.5 4.1 %collective-permute-start = (bf16[1,4,1,1024]{1,0,3,2:T(2,128)(2,1)S(1)}, bf16[1,4,1,1024]{1,0,3,2:T(2,128)(2,1)S(1)}, u32[]{:S(2)}, u32[]{:S(2)}) collective-permute-start(bf16[1,4,1,1024]{1,0,3,2:T(2,128)(2,1)S(1)} %copy.14), channel_id=1, source_target_pairs={{0,1},{1,2},{2,3},{3,4},{4,5},{5,6},{6,7},{7,8},{8,9},{9,10},{10,1... | collective-permute-start | bytes 24584 | tf_op jit(solution)/shard_map/ppermute | solution.py:20
  13.5 15.7 %copy.15 = bf16[1,4,24,1024]{1,0,3,2:T(2,128)(2,1)} copy(bf16[1,4,24,1024]{3,2,1,0:T(8,128)(2,1)} %param.4) | data formatting | bytes 393216 | tf_op args[0]
  29.2 0.0 copy-done.2
  29.2 0.0 collective-permute-done
  29.2 0.0 copy-done.1
  29.2 31.0 %tanh_convert_fusion = bf16[1,64,12,512]{1,0,3,2:T(2,128)(2,1)S(1)} fusion(bf16[64,4,3,3]{0,1,3,2:T(4,128)(2,1)S(1)} %copy-done.1, bf16[1,4,24,1024]{1,0,3,2:T(2,128)(2,1)} %copy.15, bf16[1,4,1,1024]{1,0,3,2:T(2,128)(2,1)S(1)} %collective-permute-done), kind=kOutput, calls=%fused_computation.3 | convolution fusion | flops 29095936 | bytes 995840 | tf_op jit(solution)/shard_map/conv_general_dilated | solution.py:232
  60.3 0.2 copy.17
  60.5 1.3 copy.16
  61.8 168.2 %all-gather.3.cloned.1.call-done = bf16[512,3,2304]{2,1,0:T(4,128)(2,1)} async-done(((bf16[1,3,2304]{2,1,0:T(4,128)(2,1)}), bf16[512,3,2304]{2,1,0:T(4,128)(2,1)}) %all-gather.3.cloned.1.call-update) | async-done | bytes 7077904 | tf_op jit(solution)/shard_map/all_gather | solution.py:227
  229.9 17.0 %reshape.15 = bf16[1536,2304]{1,0:T(8,128)(2,1)} reshape(bf16[512,3,2304]{2,1,0:T(4,128)(2,1)} %all-gather.3.cloned.1.call-done) | data formatting | bytes 14155776
  246.9 6.1 %convolution_convert_fusion.proj_ref = bf16[256,2304]{1,0:T(8,128)(2,1)} fusion(bf16[1536,2304]{1,0:T(8,128)(2,1)} %reshape.15, bf16[192,8,2,128]{3,2,1,0:T(2,128)(2,1)S(1)} %bitcast.17), kind=kOutput, calls=%fused_computation.2 | convolution fusion | flops 1812529152 | bytes 9043968 | tf_op jit(solution)/shard_map/dot_general | solution.py:248
  253.0 0.7 pad.9.decay_ref
  253.7 32.0 %attend.1 = bf16[256,768]{1,0:T(8,128)(2,1)} custom-call(bf16[256,2304]{1,0:T(8,128)(2,1)} %convolution_convert_fusion.proj_ref, f32[8,128]{1,0:T(8,128)} %pad.9.decay_ref), custom_call_target="tpu_custom_call" | custom-call | tf_op jit(solution)/shard_map/attend/pallas_call | solution.py:193
  285.6 1.8 copy.24
  (1 shorter events, 0.0 us)
Async XLA Ops:
  6.5 0.9 copy-start
  6.5 22.7 %copy-start.2 = (f32[1,6]{1,0:T(1,128)S(1)}, f32[1,6]{1,0:T(1,128)}, u32[]{:S(2)}) copy-start(f32[1,6]{1,0:T(1,128)} %param.7) | copy-start | bytes 76
  6.5 22.7 %copy-start.1 = (bf16[64,4,3,3]{0,1,3,2:T(4,128)(2,1)S(1)}, bf16[64,4,3,3]{0,1,3,2:T(4,128)(2,1)}, u32[]{:S(2)}) copy-start(bf16[64,4,3,3]{0,1,3,2:T(4,128)(2,1)} %param.5) | copy-start | bytes 13828
  6.5 223.4 %all-gather.3.cloned.1.call-start = ((), (), s32[]{:S(2)}) async-start(), calls=%async_computation | async-start | bytes 9455616 | tf_op jit(solution)/shard_map/all_gather | solution.py:227
  9.5 19.8 %collective-permute-start = (bf16[1,4,1,1024]{1,0,3,2:T(2,128)(2,1)S(1)}, bf16[1,4,1,1024]{1,0,3,2:T(2,128)(2,1)S(1)}, u32[]{:S(2)}, u32[]{:S(2)}) collective-permute-start(bf16[1,4,1,1024]{1,0,3,2:T(2,128)(2,1)S(1)} %copy.14), channel_id=1, source_target_pairs={{0,1},{1,2},{2,3},{3,4},{4,5},{5,6},{6,7},{7,8},{8,9},{9,10},{10,1... | collective-permute-start | bytes 24584 | tf_op jit(solution)/shard_map/ppermute | solution.py:20
Sparse Core Ops, SparseCore 0:
  11.9 218.0 all-gather.2

commit v2 on v0

v2 whole, which is shorter than its diff:
```python
import jax
import jax.numpy as jnp
from jax import lax
from jax.experimental import pallas as pl
from jax.experimental.pallas import tpu as pltpu
from jax.sharding import PartitionSpec as P

HEADS = 6
HALF = 3
DH = 128
ROW = 16
SIDE = 4
ZS = 16
SHARE = 24
WIDE = HALF * DH
COLS = 3 * WIDE
DEPTH = 48
MESH = pl.DeviceIdType.MESH
BF = jnp.bfloat16
F32 = jnp.float32


def remote(src, dst, send, recv, where):
    return pltpu.make_async_remote_copy(
        src_ref=src,
        dst_ref=dst,
        send_sem=send,
        recv_sem=recv,
        device_id=where,
        device_id_type=MESH,
    )


def one_hot(rows, columns, target, axis):
    places = lax.broadcasted_iota(jnp.int32, (rows, columns), axis)
    return jnp.where(places == target, 1.0, 0.0).astype(BF)


def kernel(
    video_ref,
    last_ref,
    w_ref,
    stem_ref,
    decay_ref,
    out_ref,
    images,
    wbuf,
    spread,
    stem,
    tokens,
    projected,
    rates,
    pair_rate,
    kv_buf,
    parts,
    pair_kv,
    scan_kv,
    scan_rate,
    state_share,
    state_buf,
    mixed_out,
    mixed_in,
    near_sems,
    main_send,
    main_recv,
    last_send,
    last_recv,
    own_sems,
    pass_sems,
    swap_sems,
    row_sems,
    rate_sems,
    scan_sems,
    state_sems,
):
    tm = lax.axis_index("tm")
    row = lax.axis_index("row")
    z, c = tm // 2, lax.rem(tm, 2)
    x, y = row // SIDE, lax.rem(row, SIDE)
    sibling = tm + 1 - 2 * c
    other = 1 - c
    below = lax.rem(row + 1, ROW)
    above = lax.rem(row + ROW - 1, ROW)
    parity = lax.rem(row, 2)
    block = row // 2
    last_parity = lax.rem(x, 2)

    barrier = pltpu.get_barrier_semaphore()

    def greet(where):
        pl.semaphore_signal(barrier, inc=1, device_id=where, device_id_type=MESH)

    def later_z(d):
        return lax.rem(z + d, ZS)

    def earlier_z(d):
        return lax.rem(z - d + ZS, ZS)

    for d in range(ZS):
        for t in range(2):
            if d > 0:
                greet({"tm": 2 * later_z(d) + t})
    greet({"tm": sibling})
    for d in range(1, ROW):
        greet({"row": lax.rem(row + d, ROW)})
    greet({"tm": sibling, "row": below})
    greet({"tm": sibling, "row": above})

    def source(b, t):
        part = b // HALF
        start = part * HEADS * DH + t * WIDE + (b - part * HALF) * DH
        return w_ref.at[:, pl.ds(pl.multiple_of(start, DH), DH)]

    def place(zi, ci, b):
        return wbuf.at[zi, ci, :, pl.ds(pl.multiple_of(b * DH, DH), DH)]

    pl.semaphore_wait(barrier, 2 * ZS - 1 + ROW - 1 + 2)

    near = [
        remote(video_ref, images.at[c, 0:96], near_sems.at[0, 0], near_sems.at[1, 0], {"tm": sibling}),
        remote(last_ref, images.at[c, 96:112], near_sems.at[0, 1], near_sems.at[1, 1], {"row": below}),
        remote(
            last_ref,
            images.at[c, 96:112],
            near_sems.at[0, 2],
            near_sems.at[1, 2],
            {"tm": sibling, "row": below},
        ),
        remote(decay_ref, rates.at[c], near_sems.at[0, 3], near_sems.at[1, 3], {"tm": sibling}),
    ]
    for copy in near:
        copy.start()

    def scatter(b, send, recv):
        copies = []
        for d in range(1, ZS):
            for t in range(2):
                copies.append(
                    remote(
                        source(b, t),
                        place(z, c, b),
                        send.at[t, d],
                        recv.at[d],
                        {"tm": 2 * later_z(d) + t},
                    )
                )
        copies.append(
            remote(source(b, other), place(z, c, b), send.at[0, 0], recv.at[0], {"tm": sibling})
        )
        return copies

    def arrived(b, ci, recv, zi):
        d = lax.rem(z - zi + ZS, ZS)

        @pl.when(jnp.logical_or(d != 0, c != ci))
        def _():
            remote(source(b, 0), place(zi, ci, b), recv.at[d], recv.at[d], {"tm": sibling}).wait_recv()

    last_block = 8

    @pl.when(c == parity)
    def _():
        for copy in scatter(block, main_send, main_recv):
            copy.start()
        wbuf[z, c, :, pl.ds(pl.multiple_of(block * DH, DH), DH)] = source(block, c)[...]

    @pl.when(c == last_parity)
    def _():
        for copy in scatter(last_block, last_send, last_recv):
            copy.start()
        wbuf[z, c, :, last_block * DH : (last_block + 1) * DH] = source(last_block, c)[...]

    images[c, 0:96, :] = video_ref[...]
    rates[c] = decay_ref[...]
    copies_of = lax.broadcasted_iota(jnp.int32, (1, 1536), 1)
    channel = copies_of // 24
    position = copies_of - channel * 24
    repeat = one_hot(64, 1536, channel, 0)
    kernels = jnp.dot(stem_ref[...], repeat, preferred_element_type=F32)
    for ij in range(24):
        spread[ij * 48 : (ij + 1) * 48, :] = jnp.where(position == ij, kernels, 0.0).astype(BF)
    term = lax.broadcasted_iota(jnp.int32, (1, 1152), 1)
    ij = term // 48
    fab = term - ij * 48
    i, j = ij // 4, ij - (ij // 4) * 4
    f = fab // 9
    a = (fab - f * 9) // 3
    b = fab - f * 9 - a * 3
    goal = jnp.where(fab < 36, (2 * j + b) * 64 + f * 16 + 2 * i + a, -1)
    chosen = one_hot(576, 1152, goal, 0)
    for n in range(3):
        stem[:, n * 512 : (n + 1) * 512] = jnp.dot(
            chosen, spread[:, n * 512 : (n + 1) * 512], preferred_element_type=F32
        ).astype(BF)

    for copy in near:
        copy.wait()

    line = lax.broadcasted_iota(jnp.int32, (128, 1), 0)
    patch, field, tap = line // 64, lax.rem(line, 64) // 16, lax.rem(line, 16)
    image_row = 12 * patch - 1 + tap
    above_row = jnp.where(row == 0, -1, 96 + field)
    picked = jnp.where(image_row < 0, above_row, field * 24 + image_row)
    picked = jnp.where(tap > 12, -1, picked)
    row_pick = one_hot(128, 112, picked, 1)
    column = lax.broadcasted_iota(jnp.int32, (1, 1152), 1)
    tap_column = 8 * lax.rem(column, 128) - 1 + column // 128
    column_pick = one_hot(1024, 1152, tap_column, 0)
    pair_rate[...] = rates[0] * rates[1]
    for frame in range(2):
        rows_of = jnp.dot(row_pick, images[frame], preferred_element_type=F32).astype(BF)
        taps = jnp.dot(rows_of, column_pick, preferred_element_type=F32).astype(BF)
        for p in range(2):
            stacked = jnp.concatenate(
                [taps[p * 64 : (p + 1) * 64, k * 128 : (k + 1) * 128] for k in range(9)], axis=0
            )
            at = (frame * 2 + p) * 128
            for n in range(3):
                made = lax.dot_general(
                    stacked,
                    stem[:, n * 512 : (n + 1) * 512],
                    (((0,), (0,)), ((), ())),
                    preferred_element_type=F32,
                )
                tokens[at : at + 128, n * 512 : (n + 1) * 512] = jnp.tanh(made).astype(BF)

    def piece(quad, chip, start, count):
        return wbuf.at[
            pl.ds(quad * 4 + start, count),
            lax.rem(chip, 2),
            :,
            pl.ds(pl.multiple_of((chip // 2) * DH, DH), DH),
        ]

    def chip_at(dx, dy):
        return lax.rem(x + dx + SIDE, SIDE) * SIDE + lax.rem(y + dy + SIDE, SIDE)

    def step(axis, d):
        return chip_at(d, 0) if axis == 0 else chip_at(0, d)

    sent = []

    def send_own(k):
        quad = lax.rem(z // 4 + k, 4)
        for o in range(4):
            arrived(block, parity, main_recv, quad * 4 + o)
        for d in range(1, SIDE):
            for axis in range(2):
                copy = remote(
                    piece(quad, row, 0, 4),
                    piece(quad, row, 0, 4),
                    own_sems.at[0, k, axis, d],
                    own_sems.at[1, k, axis, d],
                    {"row": step(axis, d)},
                )
                copy.start()
                sent.append(copy)

    def pass_on(k):
        quad = lax.rem(z // 4 + k, 4)
        for e in range(1, SIDE):
            for axis in range(2):
                origin = step(axis, -e)
                here = piece(quad, origin, 0, 4)
                remote(
                    here, here, own_sems.at[0, k, axis, e], own_sems.at[1, k, axis, e], {"row": origin}
                ).wait_recv()
                half = piece(quad, origin, 2 * axis, 2)
                for d in range(1, SIDE):
                    copy = remote(
                        half,
                        half,
                        pass_sems.at[0, k, axis, d, e],
                        pass_sems.at[1, k, axis, d, e],
                        {"row": step(1 - axis, d)},
                    )
                    copy.start()
                    sent.append(copy)

    send_own(0)
    for k in range(1, 4):
        send_own(k)
        pass_on(k - 1)
    pass_on(3)

    for zi in range(ZS):
        arrived(last_block, last_parity, last_recv, zi)
    mine = wbuf.at[:, last_parity, :, last_block * DH : (last_block + 1) * DH]
    neighbour = (x + 1 - 2 * last_parity) * SIDE + y
    swap = remote(mine, mine, swap_sems.at[0], swap_sems.at[1], {"row": neighbour})
    swap.start()

    for k in range(4):
        quad = lax.rem(z // 4 + k, 4)
        for axis in range(2):
            for d in range(1, SIDE):
                for e in range(1, SIDE):
                    origin = chip_at(-e, -d) if axis == 0 else chip_at(-d, -e)
                    half = piece(quad, origin, 2 * axis, 2)
                    remote(
                        half,
                        half,
                        pass_sems.at[0, k, axis, d, e],
                        pass_sems.at[1, k, axis, d, e],
                        {"row": origin},
                    ).wait_recv()
    swap.wait_send()
    theirs = wbuf.at[:, 1 - last_parity, :, last_block * DH : (last_block + 1) * DH]
    remote(theirs, theirs, swap_sems.at[0], swap_sems.at[1], {"row": neighbour}).wait_recv()
    for copy in sent:
        copy.wait_send()

    def project(part):
        weights = wbuf[:, :, :, part * WIDE : (part + 1) * WIDE].reshape(1536, WIDE)
        projected[:, part * WIDE : (part + 1) * WIDE] = jnp.dot(
            tokens[...], weights, preferred_element_type=F32
        ).astype(BF)

    project(1)
    project(2)

    sums = []
    for frame in range(2):
        heads = []
        for h in range(HALF):
            keys = projected[frame * 256 : (frame + 1) * 256, WIDE + h * DH : WIDE + (h + 1) * DH]
            values = projected[
                frame * 256 : (frame + 1) * 256, 2 * WIDE + h * DH : 2 * WIDE + (h + 1) * DH
            ]
            heads.append(
                lax.dot_general(
                    keys, values, (((0,), (0,)), ((), ())), preferred_element_type=F32
                )
            )
        sums.append(jnp.concatenate(heads, axis=0).reshape(ROW, SHARE, DH))
    kv_buf[...] = jnp.concatenate(sums, axis=1).astype(BF)

    reduces = []
    for d in range(1, ROW):
        peer = lax.rem(row + d, ROW)
        copy = remote(
            kv_buf.at[peer], parts.at[d], row_sems.at[0, d], row_sems.at[1, d], {"row": peer}
        )
        copy.start()
        reduces.append(copy)
    rate_copies = []
    for d in range(1, ZS):
        copy = remote(
            pair_rate,
            scan_rate.at[d],
            rate_sems.at[0, d],
            rate_sems.at[1, d],
            {"tm": 2 * later_z(d) + c},
        )
        copy.start()
        rate_copies.append(copy)

    project(0)

    head = HALF * c + (row * SHARE + lax.broadcasted_iota(jnp.int32, (SHARE, DH), 0)) // DH

    def expand(tile):
        factor = jnp.zeros((SHARE, DH), F32)
        for h in range(HEADS):
            factor = jnp.where(head == h, tile[h : h + 1, :], factor)
        return factor

    summed = kv_buf[row].astype(F32)
    for d in range(1, ROW):
        reduces[d - 1].wait()
        summed = summed + parts[d].astype(F32)
    first, second = summed[:SHARE], summed[SHARE:]
    first_rate, second_rate = expand(rates[0]), expand(rates[1])
    pair_kv[...] = (second_rate * first + second).astype(BF)
    scans = []
    for d in range(1, ZS):
        copy = remote(
            pair_kv,
            scan_kv.at[d],
            scan_sems.at[0, d],
            scan_sems.at[1, d],
            {"tm": 2 * later_z(d) + c},
        )
        copy.start()
        scans.append(copy)
    for copy in rate_copies:
        copy.wait()
    for copy in scans:
        copy.wait()

    def advance(zi, running):
        d = z - zi
        return expand(scan_rate[d]) * running + scan_kv[d].astype(F32)

    running = lax.fori_loop(0, z, advance, jnp.zeros((SHARE, DH), F32))
    first_state = first_rate * running + first
    second_state = second_rate * first_state + second
    state_share[...] = jnp.concatenate([first_state, second_state], axis=0).astype(BF)

    gathers = []
    for d in range(1, ROW):
        copy = remote(
            state_share,
            state_buf.at[row],
            state_sems.at[0, d],
            state_sems.at[1, d],
            {"row": lax.rem(row + d, ROW)},
        )
        copy.start()
        gathers.append(copy)
    state_buf[row] = state_share[...]
    for d in range(1, ROW):
        sender = lax.rem(row - d + ROW, ROW)
        remote(
            state_share,
            state_buf.at[sender],
            state_sems.at[0, d],
            state_sems.at[1, d],
            {"row": sender},
        ).wait_recv()

    states = state_buf[...].astype(F32)
    by_frame = [
        states[:, :SHARE].reshape(WIDE, DH).astype(BF),
        states[:, SHARE:].reshape(WIDE, DH).astype(BF),
    ]
    base = pl.multiple_of(c * WIDE, DH)

    def attended(frame, h):
        queries = projected[frame * 256 : (frame + 1) * 256, h * DH : (h + 1) * DH]
        found = jnp.dot(
            queries, by_frame[frame][h * DH : (h + 1) * DH, :], preferred_element_type=F32
        )
        scale = lax.rsqrt(jnp.mean(found * found, axis=-1, keepdims=True) + 1e-06)
        return (found * scale).astype(BF)

    for frame in range(2):
        for h in range(HALF):
            mixed_out[frame, :, h * DH : (h + 1) * DH] = attended(frame, h)
    final = remote(
        mixed_out.at[other], mixed_in, near_sems.at[0, 4], near_sems.at[1, 4], {"tm": sibling}
    )
    final.start()
    out_ref[:, pl.ds(base, WIDE)] = mixed_out[c]

    @pl.when(c == parity)
    def _():
        for copy in scatter(block, main_send, main_recv):
            copy.wait_send()

    @pl.when(c == last_parity)
    def _():
        for copy in scatter(last_block, last_send, last_recv):
            copy.wait_send()

    for copy in gathers:
        copy.wait_send()
    final.wait()
    out_ref[:, pl.ds(pl.multiple_of(other * WIDE, DH), WIDE)] = mixed_in[...]


def run(video, last, weights, stem, decay_tile):
    dma = pltpu.SemaphoreType.DMA
    vmem = pltpu.VMEM
    return pl.pallas_call(
        kernel,
        out_shape=jax.ShapeDtypeStruct((256, HEADS * DH), BF),
        in_specs=[pl.BlockSpec(memory_space=pltpu.VMEM)] * 5,
        out_specs=pl.BlockSpec(memory_space=pltpu.VMEM),
        scratch_shapes=[
            vmem((2, 112, 1024), BF),
            vmem((ZS, 2, DEPTH, COLS), BF),
            vmem((1152, 1536), BF),
            vmem((576, 1536), BF),
            vmem((512, 1536), BF),
            vmem((512, COLS), BF),
            vmem((2, 8, 128), F32),
            vmem((8, 128), F32),
            vmem((ROW, 2 * SHARE, DH), BF),
            vmem((ROW, 2 * SHARE, DH), BF),
            vmem((SHARE, DH), BF),
            vmem((ZS, SHARE, DH), BF),
            vmem((ZS, 8, 128), F32),
            vmem((2 * SHARE, DH), BF),
            vmem((ROW, 2 * SHARE, DH), BF),
            vmem((2, 256, WIDE), BF),
            vmem((256, WIDE), BF),
            dma((2, 5)),
            dma((2, ZS)),
            dma((ZS,)),
            dma((2, ZS)),
            dma((ZS,)),
            dma((2, 4, 2, SIDE)),
            dma((2, 4, 2, SIDE, SIDE)),
            dma((2,)),
            dma((2, ROW)),
            dma((2, ZS)),
            dma((2, ZS)),
            dma((2, ROW)),
        ],
        compiler_params=pltpu.CompilerParams(collective_id=0, has_side_effects=True),
        name="frames",
    )(video, last, weights, stem, decay_tile)


def local(video, stem_weight, w_qkv, decay):
    image = video.reshape(96, 1024)
    last = jnp.pad(video[0, :, -1, :], ((0, 12), (0, 0)))
    stem = jnp.pad(stem_weight.reshape(64, 36).T, ((0, 12), (0, 0)))
    decay_tile = jnp.pad(jnp.broadcast_to(decay.reshape(HEADS, 1), (HEADS, 128)), ((0, 2), (0, 0)))
    mixed = run(image, last, w_qkv, stem, decay_tile)
    return mixed.reshape(1, 2, 128, HEADS * DH)


def solution(mesh):
    return jax.shard_map(
        local,
        mesh=mesh,
        in_specs=(P("tm", None, "row", None), P(), P("tm", None), P("tm", None)),
        out_specs=P("tm", "row", None, None),
        check_vma=False,
    )
```

time: 326 us -> 97 us (0.30)
  the two profiles are of different devices: /device:TPU:481 before, /device:TPU:1 now
where the time goes in v2:
time: 97 us; the launch traced here: 96.8 us
  Pallas kernels  91.5 us (94%)
  local copies, waits for them, and re-layouts  5.22 us (5%)
    pallas_call x1, Pallas kernels, run(): pl.pallas_call(kernel, out_shape=jax.ShapeDtypeStruct((256, HEADS * DH),...  91.5 us

profile of v2, /device:TPU:1, one launch (start us, length us, event | category | flops | bytes accessed | tf_op | source)
XLA Modules:
  0.0 96.8 jit_solution(5175850622609941756)
XLA Ops:
  0.0 0.0 copy-start
  0.0 0.7 pad.16
  0.7 0.7 pad.17.decay_ref
  1.3 0.0 copy-done
  1.4 0.6 pad.15.stem_ref
  2.0 0.9 slice.3
  2.9 0.6 pad.14.last_ref
  3.5 91.5 %frames.1 = bf16[256,768]{1,0:T(8,128)(2,1)} custom-call(bf16[96,1024]{1,0:T(8,128)(2,1)} %bitcast.10, bf16[16,1024]{1,0:T(8,128)(2,1)} %pad.14.last_ref, bf16[48,2304]{1,0:T(8,128)(2,1)} %w_ref.1, bf16[48,64]{1,0:T(8,128)(2,1)} %pad.15.stem_ref, f32[8,128]{1,0:T(8,128)} %pad.17.decay_ref), custom_call_target="tpu_custom_call" | custom-call | tf_op jit(solution)/shard_map/frames/pallas_call | solution.py:465
  95.0 1.8 %copy.13 = bf16[1,2,128,768]{3,2,1,0:T(8,128)(2,1)} copy(bf16[1,2,128,768]{3,2,1,0:T(8,128)(2,1)} %bitcast.9) | data formatting | bytes 786432
  (3 shorter events, 0.0 us)
Async XLA Ops:
  0.0 1.3 %copy-start = (bf16[64,4,3,3]{0,1,3,2:T(4,128)(2,1)S(1)}, bf16[64,4,3,3]{0,1,3,2:T(4,128)(2,1)}, u32[]{:S(2)}) copy-start(bf16[64,4,3,3]{0,1,3,2:T(4,128)(2,1)} %param.5) | copy-start | bytes 13828

commit v3 on v2

--- a/solution.py
+++ b/solution.py
@@ -37,13 +37,14 @@
 
 
 def kernel(
+    decay_ref,
     video_ref,
-    last_ref,
     w_ref,
     stem_ref,
-    decay_ref,
     out_ref,
     images,
+    last_rows,
+    own_rate,
     wbuf,
     spread,
     stem,
@@ -61,10 +62,10 @@
     mixed_out,
     mixed_in,
     near_sems,
-    main_send,
-    main_recv,
-    last_send,
-    last_recv,
+    main_sems,
+    main_next,
+    last_sems,
+    last_next,
     own_sems,
     pass_sems,
     swap_sems,
@@ -96,10 +97,10 @@
     def earlier_z(d):
         return lax.rem(z - d + ZS, ZS)
 
-    for d in range(ZS):
-        for t in range(2):
-            if d > 0:
-                greet({"tm": 2 * later_z(d) + t})
+    for d in range(1, ZS):
+        greet({"tm": 2 * later_z(d) + c})
+    for d in (4, 8, 12):
+        greet({"tm": 2 * later_z(d) + other})
     greet({"tm": sibling})
     for d in range(1, ROW):
         greet({"row": lax.rem(row + d, ROW)})
@@ -112,66 +113,102 @@
         return w_ref.at[:, pl.ds(pl.multiple_of(start, DH), DH)]
 
     def place(zi, ci, b):
-        return wbuf.at[zi, ci, :, pl.ds(pl.multiple_of(b * DH, DH), DH)]
-
-    pl.semaphore_wait(barrier, 2 * ZS - 1 + ROW - 1 + 2)
+        return wbuf.at[
+            zi // 4, lax.rem(zi, 4), ci, :, pl.ds(pl.multiple_of(b * DH, DH), DH)
+        ]
+
+    line = lax.broadcasted_iota(jnp.int32, (16, 1), 0)
+    last_pick = one_hot(16, 96, jnp.where(line < 4, 24 * line + 23, -1), 1)
+    last_rows[...] = jnp.dot(last_pick, video_ref[...], preferred_element_type=F32).astype(BF)
+    place_of = lax.broadcasted_iota(jnp.int32, (8, 128), 0)
+    rate = jnp.zeros((8, 128), F32)
+    for h in range(HEADS):
+        rate = jnp.where(place_of == h, decay_ref[0, h], rate)
+    own_rate[...] = rate
+    rates[c] = rate
+
+    pl.semaphore_wait(barrier, ZS - 1 + 3 + 1 + ROW - 1 + 2)
 
     near = [
         remote(video_ref, images.at[c, 0:96], near_sems.at[0, 0], near_sems.at[1, 0], {"tm": sibling}),
-        remote(last_ref, images.at[c, 96:112], near_sems.at[0, 1], near_sems.at[1, 1], {"row": below}),
+        remote(last_rows, images.at[c, 96:112], near_sems.at[0, 1], near_sems.at[1, 1], {"row": below}),
         remote(
-            last_ref,
+            last_rows,
             images.at[c, 96:112],
             near_sems.at[0, 2],
             near_sems.at[1, 2],
             {"tm": sibling, "row": below},
         ),
-        remote(decay_ref, rates.at[c], near_sems.at[0, 3], near_sems.at[1, 3], {"tm": sibling}),
+        remote(own_rate, rates.at[c], near_sems.at[0, 3], near_sems.at[1, 3], {"tm": sibling}),
     ]
     for copy in near:
         copy.start()
 
-    def scatter(b, send, recv):
+    def scatter(b, sems):
         copies = []
-        for d in range(1, ZS):
+        for k in range(1, 4):
             for t in range(2):
                 copies.append(
                     remote(
                         source(b, t),
                         place(z, c, b),
-                        send.at[t, d],
-                        recv.at[d],
-                        {"tm": 2 * later_z(d) + t},
+                        sems.at[0, t, k],
+                        sems.at[1, 0, k],
+                        {"tm": 2 * later_z(4 * k) + t},
                     )
                 )
         copies.append(
-            remote(source(b, other), place(z, c, b), send.at[0, 0], recv.at[0], {"tm": sibling})
+            remote(
+                source(b, other), place(z, c, b), sems.at[0, 0, 0], sems.at[1, 0, 0], {"tm": sibling}
+            )
         )
         return copies
 
-    def arrived(b, ci, recv, zi):
-        d = lax.rem(z - zi + ZS, ZS)
-
-        @pl.when(jnp.logical_or(d != 0, c != ci))
+    def scattered(b, ci, sems):
+        for k in range(1, 4):
+            spot = place(earlier_z(4 * k), ci, b)
+            remote(spot, spot, sems.at[0, 0, k], sems.at[1, 0, k], {"tm": sibling}).wait_recv()
+
+        @pl.when(c != ci)
         def _():
-            remote(source(b, 0), place(zi, ci, b), recv.at[d], recv.at[d], {"tm": sibling}).wait_recv()
+            spot = place(z, ci, b)
+            remote(spot, spot, sems.at[0, 0, 0], sems.at[1, 0, 0], {"tm": sibling}).wait_recv()
+
+    def column_of(member, ci, b):
+        return wbuf.at[:, member, ci, :, pl.ds(pl.multiple_of(b * DH, DH), DH)]
+
+    member = lax.rem(z, 4)
+    hops = (0, 1, 15, 2)
+
+    def hand_on(b, ci, sems):
+        copies = []
+        for k in range(1, 4):
+            own = column_of(member, ci, b)
+            copies.append(
+                remote(own, own, sems.at[0, k], sems.at[1, k], {"tm": 2 * later_z(hops[k]) + c})
+            )
+        return copies
+
+    def member_of(k):
+        return lax.rem(z - hops[k] + ZS, 4)
+
+    def handed(b, ci, sems, k):
+        spot = column_of(member_of(k), ci, b)
+        remote(spot, spot, sems.at[0, k], sems.at[1, k], {"tm": sibling}).wait_recv()
 
     last_block = 8
 
     @pl.when(c == parity)
     def _():
-        for copy in scatter(block, main_send, main_recv):
+        for copy in scatter(block, main_sems):
             copy.start()
-        wbuf[z, c, :, pl.ds(pl.multiple_of(block * DH, DH), DH)] = source(block, c)[...]
+        place(z, c, block)[...] = source(block, c)[...]
 
     @pl.when(c == last_parity)
     def _():
-        for copy in scatter(last_block, last_send, last_recv):
-            copy.start()
-        wbuf[z, c, :, last_block * DH : (last_block + 1) * DH] = source(last_block, c)[...]
+        place(z, c, last_block)[...] = source(last_block, c)[...]
 
     images[c, 0:96, :] = video_ref[...]
-    rates[c] = decay_ref[...]
     copies_of = lax.broadcasted_iota(jnp.int32, (1, 1536), 1)
     channel = copies_of // 24
     position = copies_of - channel * 24
@@ -192,6 +229,69 @@
         stem[:, n * 512 : (n + 1) * 512] = jnp.dot(
             chosen, spread[:, n * 512 : (n + 1) * 512], preferred_element_type=F32
         ).astype(BF)
+
+    def piece(k, chip, start, count):
+        return wbuf.at[
+            start : start + count,
+            member_of(k),
+            lax.rem(chip, 2),
+            :,
+            pl.ds(pl.multiple_of((chip // 2) * DH, DH), DH),
+        ]
+
+    def chip_at(dx, dy):
+        return lax.rem(x + dx + SIDE, SIDE) * SIDE + lax.rem(y + dy + SIDE, SIDE)
+
+    def step(axis, d):
+        return chip_at(d, 0) if axis == 0 else chip_at(0, d)
+
+    sent = []
+
+    def send_own(k):
+        if k > 0:
+            handed(block, parity, main_next, k)
+        for d in range(1, SIDE):
+            for axis in range(2):
+                copy = remote(
+                    piece(k, row, 0, 4),
+                    piece(k, row, 0, 4),
+                    own_sems.at[0, k, axis, d],
+                    own_sems.at[1, k, axis, d],
+                    {"row": step(axis, d)},
+                )
+                copy.start()
+                sent.append(copy)
+
+    def pass_on(k):
+        for e in range(1, SIDE):
+            for axis in range(2):
+                origin = step(axis, -e)
+                here = piece(k, origin, 0, 4)
+                remote(
+                    here, here, own_sems.at[0, k, axis, e], own_sems.at[1, k, axis, e], {"row": origin}
+                ).wait_recv()
+                half = piece(k, origin, 2 * axis, 2)
+                for d in range(1, SIDE):
+                    copy = remote(
+                        half,
+                        half,
+                        pass_sems.at[0, k, axis, d, e],
+                        pass_sems.at[1, k, axis, d, e],
+                        {"row": step(1 - axis, d)},
+                    )
+                    copy.start()
+                    sent.append(copy)
+
+    scattered(block, parity, main_sems)
+    handing = hand_on(block, parity, main_next)
+    for copy in handing:
+        copy.start()
+    send_own(0)
+
+    @pl.when(c == last_parity)
+    def _():
+        for copy in scatter(last_block, last_sems):
+            copy.start()
 
     for copy in near:
         copy.wait()
@@ -224,79 +324,30 @@
                 )
                 tokens[at : at + 128, n * 512 : (n + 1) * 512] = jnp.tanh(made).astype(BF)
 
-    def piece(quad, chip, start, count):
-        return wbuf.at[
-            pl.ds(quad * 4 + start, count),
-            lax.rem(chip, 2),
-            :,
-            pl.ds(pl.multiple_of((chip // 2) * DH, DH), DH),
-        ]
-
-    def chip_at(dx, dy):
-        return lax.rem(x + dx + SIDE, SIDE) * SIDE + lax.rem(y + dy + SIDE, SIDE)
-
-    def step(axis, d):
-        return chip_at(d, 0) if axis == 0 else chip_at(0, d)
-
-    sent = []
-
-    def send_own(k):
-        quad = lax.rem(z // 4 + k, 4)
-        for o in range(4):
-            arrived(block, parity, main_recv, quad * 4 + o)
-        for d in range(1, SIDE):
-            for axis in range(2):
-                copy = remote(
-                    piece(quad, row, 0, 4),
-                    piece(quad, row, 0, 4),
-                    own_sems.at[0, k, axis, d],
-                    own_sems.at[1, k, axis, d],
-                    {"row": step(axis, d)},
-                )
-                copy.start()
-                sent.append(copy)
-
-    def pass_on(k):
-        quad = lax.rem(z // 4 + k, 4)
-        for e in range(1, SIDE):
-            for axis in range(2):
-                origin = step(axis, -e)
-                here = piece(quad, origin, 0, 4)
-                remote(
-                    here, here, own_sems.at[0, k, axis, e], own_sems.at[1, k, axis, e], {"row": origin}
-                ).wait_recv()
-                half = piece(quad, origin, 2 * axis, 2)
-                for d in range(1, SIDE):
-                    copy = remote(
-                        half,
-                        half,
-                        pass_sems.at[0, k, axis, d, e],
-                        pass_sems.at[1, k, axis, d, e],
-                        {"row": step(1 - axis, d)},
-                    )
-                    copy.start()
-                    sent.append(copy)
-
-    send_own(0)
+    send_own(1)
+    pass_on(0)
+    scattered(last_block, last_parity, last_sems)
+    last_handing = hand_on(last_block, last_parity, last_next)
+    for copy in last_handing:
+        copy.start()
+    send_own(2)
+    pass_on(1)
+    send_own(3)
+    pass_on(2)
+    pass_on(3)
     for k in range(1, 4):
-        send_own(k)
-        pass_on(k - 1)
-    pass_on(3)
-
-    for zi in range(ZS):
-        arrived(last_block, last_parity, last_recv, zi)
-    mine = wbuf.at[:, last_parity, :, last_block * DH : (last_block + 1) * DH]
+        handed(last_block, last_parity, last_next, k)
+    mine = wbuf.at[:, :, last_parity, :, last_block * DH : (last_block + 1) * DH]
     neighbour = (x + 1 - 2 * last_parity) * SIDE + y
     swap = remote(mine, mine, swap_sems.at[0], swap_sems.at[1], {"row": neighbour})
     swap.start()
 
     for k in range(4):
-        quad = lax.rem(z // 4 + k, 4)
         for axis in range(2):
             for d in range(1, SIDE):
                 for e in range(1, SIDE):
                     origin = chip_at(-e, -d) if axis == 0 else chip_at(-d, -e)
-                    half = piece(quad, origin, 2 * axis, 2)
+                    half = piece(k, origin, 2 * axis, 2)
                     remote(
                         half,
                         half,
@@ -305,13 +356,13 @@
                         {"row": origin},
                     ).wait_recv()
     swap.wait_send()
-    theirs = wbuf.at[:, 1 - last_parity, :, last_block * DH : (last_block + 1) * DH]
+    theirs = wbuf.at[:, :, 1 - last_parity, :, last_block * DH : (last_block + 1) * DH]
     remote(theirs, theirs, swap_sems.at[0], swap_sems.at[1], {"row": neighbour}).wait_recv()
-    for copy in sent:
+    for copy in sent + handing + last_handing:
         copy.wait_send()
 
     def project(part):
-        weights = wbuf[:, :, :, part * WIDE : (part + 1) * WIDE].reshape(1536, WIDE)
+        weights = wbuf[:, :, :, :, part * WIDE : (part + 1) * WIDE].reshape(1536, WIDE)
         projected[:, part * WIDE : (part + 1) * WIDE] = jnp.dot(
             tokens[...], weights, preferred_element_type=F32
         ).astype(BF)
@@ -445,12 +496,12 @@
 
     @pl.when(c == parity)
     def _():
-        for copy in scatter(block, main_send, main_recv):
+        for copy in scatter(block, main_sems):
             copy.wait_send()
 
     @pl.when(c == last_parity)
     def _():
-        for copy in scatter(last_block, last_send, last_recv):
+        for copy in scatter(last_block, last_sems):
             copy.wait_send()
 
     for copy in gathers:
@@ -459,17 +510,20 @@
     out_ref[:, pl.ds(pl.multiple_of(other * WIDE, DH), WIDE)] = mixed_in[...]
 
 
-def run(video, last, weights, stem, decay_tile):
+def run(decay, video, weights, stem):
     dma = pltpu.SemaphoreType.DMA
     vmem = pltpu.VMEM
     return pl.pallas_call(
         kernel,
         out_shape=jax.ShapeDtypeStruct((256, HEADS * DH), BF),
-        in_specs=[pl.BlockSpec(memory_space=pltpu.VMEM)] * 5,
+        in_specs=[pl.BlockSpec(memory_space=pltpu.SMEM)]
+        + [pl.BlockSpec(memory_space=pltpu.VMEM)] * 3,
         out_specs=pl.BlockSpec(memory_space=pltpu.VMEM),
         scratch_shapes=[
             vmem((2, 112, 1024), BF),
-            vmem((ZS, 2, DEPTH, COLS), BF),
+            vmem((16, 1024), BF),
+            vmem((8, 128), F32),
+            vmem((4, 4, 2, DEPTH, COLS), BF),
             vmem((1152, 1536), BF),
             vmem((576, 1536), BF),
             vmem((512, 1536), BF),
@@ -486,10 +540,10 @@
             vmem((2, 256, WIDE), BF),
             vmem((256, WIDE), BF),
             dma((2, 5)),
-            dma((2, ZS)),
-            dma((ZS,)),
-            dma((2, ZS)),
-            dma((ZS,)),
+            dma((2, 2, 4)),
+            dma((2, 4)),
+            dma((2, 2, 4)),
+            dma((2, 4)),
             dma((2, 4, 2, SIDE)),
             dma((2, 4, 2, SIDE, SIDE)),
             dma((2,)),
@@ -500,15 +554,13 @@
         ],
         compiler_params=pltpu.CompilerParams(collective_id=0, has_side_effects=True),
         name="frames",
-    )(video, last, weights, stem, decay_tile)
+    )(decay, video, weights, stem)
 
 
 def local(video, stem_weight, w_qkv, decay):
     image = video.reshape(96, 1024)
-    last = jnp.pad(video[0, :, -1, :], ((0, 12), (0, 0)))
     stem = jnp.pad(stem_weight.reshape(64, 36).T, ((0, 12), (0, 0)))
-    decay_tile = jnp.pad(jnp.broadcast_to(decay.reshape(HEADS, 1), (HEADS, 128)), ((0, 2), (0, 0)))
-    mixed = run(image, last, w_qkv, stem, decay_tile)
+    mixed = run(decay, image, w_qkv, stem)
     return mixed.reshape(1, 2, 128, HEADS * DH)
 
 

time: 97 us -> 88.1 us (0.908)
  Pallas kernels: 91.5 us -> 84.7 us
  local copies, waits for them, and re-layouts: 5.22 us -> 3.1 us
    pallas_call x1, Pallas kernels: 91.5 us -> 84.7 us  [run(): pl.pallas_call(kernel, out_shape=jax.ShapeDtypeStruct((256, HEADS * DH),...]
    pad x3 -> x0, local copies, waits for them, and re-layouts: 1.96 us -> none  [the longest x2 1.33 us: local(): jnp.pad(jnp.broadcast_to(decay.reshape(HEADS, 1), (HEADS, 128)), ((0, 2),...]
    unnamed x5 -> x2, local copies, waits for them, and re-layouts: 1.78 us -> 2.47 us
where the time goes in v3:
time: 88.1 us; the launch traced here: 87.8 us
  Pallas kernels  84.7 us (96%)
  local copies, waits for them, and re-layouts  3.1 us (4%)
    pallas_call x1, Pallas kernels, run(): pl.pallas_call(kernel, out_shape=jax.ShapeDtypeStruct((256, HEADS * DH),...  84.7 us
    unnamed x2, local copies, waits for them, and re-layouts  2.47 us

profile of v3, /device:TPU:1, one launch (start us, length us, event | category | flops | bytes accessed | tf_op | source)
XLA Modules:
  0.0 87.8 jit_solution(17444160400903783038)
XLA Ops:
  0.0 0.7 copy.6
  0.7 0.6 pad.4.stem_ref
  1.3 84.7 %frames.1 = bf16[256,768]{1,0:T(8,128)(2,1)} custom-call(f32[1,6]{1,0:T(1,128)} %decay_ref.1, bf16[96,1024]{1,0:T(8,128)(2,1)} %bitcast.6, bf16[48,2304]{1,0:T(8,128)(2,1)} %w_ref.1, bf16[48,64]{1,0:T(8,128)(2,1)} %pad.4.stem_ref), custom_call_target="tpu_custom_call" | custom-call | tf_op jit(solution)/shard_map/frames/pallas_call | solution.py:516
  86.1 1.8 %copy.8 = bf16[1,2,128,768]{3,2,1,0:T(8,128)(2,1)} copy(bf16[1,2,128,768]{3,2,1,0:T(8,128)(2,1)} %bitcast.5) | data formatting | bytes 786432
  (1 shorter events, 0.0 us)

commit v4 on v3

--- a/solution.py
+++ b/solution.py
@@ -216,20 +216,6 @@
     kernels = jnp.dot(stem_ref[...], repeat, preferred_element_type=F32)
     for ij in range(24):
         spread[ij * 48 : (ij + 1) * 48, :] = jnp.where(position == ij, kernels, 0.0).astype(BF)
-    term = lax.broadcasted_iota(jnp.int32, (1, 1152), 1)
-    ij = term // 48
-    fab = term - ij * 48
-    i, j = ij // 4, ij - (ij // 4) * 4
-    f = fab // 9
-    a = (fab - f * 9) // 3
-    b = fab - f * 9 - a * 3
-    goal = jnp.where(fab < 36, (2 * j + b) * 64 + f * 16 + 2 * i + a, -1)
-    chosen = one_hot(576, 1152, goal, 0)
-    for n in range(3):
-        stem[:, n * 512 : (n + 1) * 512] = jnp.dot(
-            chosen, spread[:, n * 512 : (n + 1) * 512], preferred_element_type=F32
-        ).astype(BF)
-
     def piece(k, chip, start, count):
         return wbuf.at[
             start : start + count,
@@ -293,6 +279,23 @@
         for copy in scatter(last_block, last_sems):
             copy.start()
 
+    term = lax.broadcasted_iota(jnp.int32, (1, 1152), 1)
+    ij = term // 48
+    fab = term - ij * 48
+    i, j = ij // 4, ij - (ij // 4) * 4
+    f = fab // 9
+    a = (fab - f * 9) // 3
+    b = fab - f * 9 - a * 3
+    goal = jnp.where(fab < 36, (2 * j + b) * 64 + f * 16 + 2 * i + a, -1)
+    chosen = one_hot(576, 1152, goal, 0)
+    for n in range(3):
+        stem[:, n * 512 : (n + 1) * 512] = jnp.dot(
+            chosen, spread[:, n * 512 : (n + 1) * 512], preferred_element_type=F32
+        ).astype(BF)
+
+    send_own(1)
+    pass_on(0)
+
     for copy in near:
         copy.wait()
 
@@ -307,7 +310,7 @@
     tap_column = 8 * lax.rem(column, 128) - 1 + column // 128
     column_pick = one_hot(1024, 1152, tap_column, 0)
     pair_rate[...] = rates[0] * rates[1]
-    for frame in range(2):
+    def embed(frame):
         rows_of = jnp.dot(row_pick, images[frame], preferred_element_type=F32).astype(BF)
         taps = jnp.dot(rows_of, column_pick, preferred_element_type=F32).astype(BF)
         for p in range(2):
@@ -324,23 +327,27 @@
                 )
                 tokens[at : at + 128, n * 512 : (n + 1) * 512] = jnp.tanh(made).astype(BF)
 
-    send_own(1)
-    pass_on(0)
+    neighbour = (x + 1 - 2 * last_parity) * SIDE + y
+
+    def swap(k, ci):
+        spot = wbuf.at[:, member_of(k), ci, :, last_block * DH : (last_block + 1) * DH]
+        return remote(spot, spot, swap_sems.at[0, k], swap_sems.at[1, k], {"row": neighbour})
+
+    embed(0)
+    send_own(2)
+    pass_on(1)
     scattered(last_block, last_parity, last_sems)
     last_handing = hand_on(last_block, last_parity, last_next)
     for copy in last_handing:
         copy.start()
-    send_own(2)
-    pass_on(1)
+    swap(0, last_parity).start()
+    embed(1)
     send_own(3)
     pass_on(2)
-    pass_on(3)
     for k in range(1, 4):
         handed(last_block, last_parity, last_next, k)
-    mine = wbuf.at[:, :, last_parity, :, last_block * DH : (last_block + 1) * DH]
-    neighbour = (x + 1 - 2 * last_parity) * SIDE + y
-    swap = remote(mine, mine, swap_sems.at[0], swap_sems.at[1], {"row": neighbour})
-    swap.start()
+        swap(k, last_parity).start()
+    pass_on(3)
 
     for k in range(4):
         for axis in range(2):
@@ -355,9 +362,9 @@
                         pass_sems.at[1, k, axis, d, e],
                         {"row": origin},
                     ).wait_recv()
-    swap.wait_send()
-    theirs = wbuf.at[:, :, 1 - last_parity, :, last_block * DH : (last_block + 1) * DH]
-    remote(theirs, theirs, swap_sems.at[0], swap_sems.at[1], {"row": neighbour}).wait_recv()
+    for k in range(4):
+        swap(k, 1 - last_parity).wait_recv()
+        swap(k, last_parity).wait_send()
     for copy in sent + handing + last_handing:
         copy.wait_send()
 
@@ -546,7 +553,7 @@
             dma((2, 4)),
             dma((2, 4, 2, SIDE)),
             dma((2, 4, 2, SIDE, SIDE)),
-            dma((2,)),
+            dma((2, 4)),
             dma((2, ROW)),
             dma((2, ZS)),
             dma((2, ZS)),

time: 88.1 us -> 88.6 us (level)
  no operation moved by 1% of the time
where the time goes in v4:
time: 88.6 us; the launch traced here: 88.3 us
  Pallas kernels  85.2 us (96%)
  local copies, waits for them, and re-layouts  3.1 us (3%)
    pallas_call x1, Pallas kernels, run(): pl.pallas_call(kernel, out_shape=jax.ShapeDtypeStruct((256, HEADS * DH),...  85.2 us
    unnamed x2, local copies, waits for them, and re-layouts  2.47 us

profile of v4, /device:TPU:1, one launch (start us, length us, event | category | flops | bytes accessed | tf_op | source)
XLA Modules:
  0.0 88.3 jit_solution(14991172370952259497)
XLA Ops:
  0.0 0.7 copy.6
  0.7 0.6 pad.4.stem_ref
  1.3 85.2 %frames.1 = bf16[256,768]{1,0:T(8,128)(2,1)} custom-call(f32[1,6]{1,0:T(1,128)} %decay_ref.1, bf16[96,1024]{1,0:T(8,128)(2,1)} %bitcast.6, bf16[48,2304]{1,0:T(8,128)(2,1)} %w_ref.1, bf16[48,64]{1,0:T(8,128)(2,1)} %pad.4.stem_ref), custom_call_target="tpu_custom_call" | custom-call | tf_op jit(solution)/shard_map/frames/pallas_call | solution.py:523
  86.6 1.8 %copy.8 = bf16[1,2,128,768]{3,2,1,0:T(8,128)(2,1)} copy(bf16[1,2,128,768]{3,2,1,0:T(8,128)(2,1)} %bitcast.5) | data formatting | bytes 786432
  (1 shorter events, 0.0 us)

commit v5 on v3

--- a/solution.py
+++ b/solution.py
@@ -213,7 +213,12 @@
     channel = copies_of // 24
     position = copies_of - channel * 24
     repeat = one_hot(64, 1536, channel, 0)
-    kernels = jnp.dot(stem_ref[...], repeat, preferred_element_type=F32)
+    stem_line = lax.broadcasted_iota(jnp.int32, (DEPTH, 1), 0)
+    stem_pick = one_hot(DEPTH, 36, stem_line, 1)
+    padded = lax.dot_general(
+        stem_pick, stem_ref[...], (((1,), (1,)), ((), ())), preferred_element_type=F32
+    ).astype(BF)
+    kernels = jnp.dot(padded, repeat, preferred_element_type=F32)
     for ij in range(24):
         spread[ij * 48 : (ij + 1) * 48, :] = jnp.where(position == ij, kernels, 0.0).astype(BF)
     term = lax.broadcasted_iota(jnp.int32, (1, 1152), 1)
@@ -559,7 +564,7 @@
 
 def local(video, stem_weight, w_qkv, decay):
     image = video.reshape(96, 1024)
-    stem = jnp.pad(stem_weight.reshape(64, 36).T, ((0, 12), (0, 0)))
+    stem = stem_weight.reshape(64, 36)
     mixed = run(decay, image, w_qkv, stem)
     return mixed.reshape(1, 2, 128, HEADS * DH)
 

time: 88.1 us -> 88.1 us (level)
  no operation moved by 1% of the time
where the time goes in v5:
time: 88.1 us; the launch traced here: 87.9 us
  Pallas kernels  84.7 us (96%)
  local copies, waits for them, and re-layouts  3.2 us (4%)
    pallas_call x1, Pallas kernels, run(): pl.pallas_call(kernel, out_shape=jax.ShapeDtypeStruct((256, HEADS * DH),...  84.7 us
    unnamed x2, local copies, waits for them, and re-layouts  2.47 us

profile of v5, /device:TPU:1, one launch (start us, length us, event | category | flops | bytes accessed | tf_op | source)
XLA Modules:
  0.0 87.9 jit_solution(4720060876854249386)
XLA Ops:
  0.0 0.7 copy.6
  0.7 0.7 copy.7.stem_ref
  1.4 84.7 %frames.1 = bf16[256,768]{1,0:T(8,128)(2,1)} custom-call(f32[1,6]{1,0:T(1,128)} %decay_ref.1, bf16[96,1024]{1,0:T(8,128)(2,1)} %bitcast.5, bf16[48,2304]{1,0:T(8,128)(2,1)} %w_ref.1, bf16[64,36]{1,0:T(8,128)(2,1)} %copy.7.stem_ref), custom_call_target="tpu_custom_call" | custom-call | tf_op jit(solution)/shard_map/frames/pallas_call | solution.py:521
  86.2 1.8 %copy.9 = bf16[1,2,128,768]{3,2,1,0:T(8,128)(2,1)} copy(bf16[1,2,128,768]{3,2,1,0:T(8,128)(2,1)} %bitcast.4) | data formatting | bytes 786432
  (1 shorter events, 0.0 us)
